TPU v7x, 32 devices: a whole 2x2x4 slice. The times are simulated.
32 devices in a mesh: leaf: 4 (over z), row: 2 (over x), top: 4 (over y, core).
Axes of the slice: x: 2, y: 2, z: 4, core: 2. Of those that a mesh axis runs over, the one named last changes fastest.
Arguments:
- loads: bfloat16 [4, 2, 4, 1, 256, 32], P('leaf', 'row', 'top'), may hold values from -6 to 6
- flux_maps: bfloat16 [4, 2, 4, 640, 256], P('leaf', 'row', 'top'), may hold values from -0.375 to 0.375
- chain_maps: float32 [4, 2, 4, 640, 640], P('leaf', 'row', 'top')
- leaf_maps: bfloat16 [4, 2, 4, 1, 256, 256], P('leaf', 'row', 'top'), may hold values from -0.375 to 0.375
- edge_maps: bfloat16 [4, 2, 4, 1, 256, 640], P('leaf', 'row', 'top'), may hold values from -0.25 to 0.25
- top_maps: bfloat16 [4, 2, 4, 1, 256, 128], P('leaf', 'row', 'top'), may hold values from -0.5 to 0.5
- slot_nodes: int32 [4, 2, 4, 128], P('leaf', 'row', 'top'), may hold values from 0 to 8191
- slot_counts: int32 [4, 2, 4], P('leaf', 'row', 'top'), may hold values from 1 to 128, 320 in all within a row
- top_loads: float32 [8192, 32], P('leaf'), may hold values from -6 to 6
- top_inverse: float32 [8192, 8192], P('top', ('leaf', 'row')), may hold values from -0.0625 to 0.0625
Outputs:
- solution: bfloat16 [4, 2, 4, 1, 256, 32], P('leaf', 'row', 'top')
- top_values: float32 [8192, 32], P('top')
Inputs may be any that keep to these rules, and one draw needn't show every extreme that they name: `slot_counts`: over the 4 subtrees of one x-y cell (same x and y, all t) the live slots sum to 320, and one of those subtrees has all 128 slots live.
All inputs are finite; a program needn't handle non-finite values. No bound on the sum of `slot_counts` on one device may be relied on, other than what follows from the above.
Results may differ from a plain program's by a relative error of at most 0.0046.
Values sent between devices are 32-bit elements; how exact they have to be, the bound alone decides.
A program may use at most 64 MiB of HBM per device.

v0:
```python
import jax
import jax.numpy as jnp
from jax import lax
from jax.sharding import PartitionSpec as P


def passed_along(value, axis, steps):
    count = lax.axis_size(axis)
    first, last = (max(0, -steps), min(count, count - steps))
    return lax.ppermute(value, axis, [(source, source + steps) for source in range(first, last)])


def body(
    loads,
    flux_maps,
    chain_maps,
    leaf_maps,
    edge_maps,
    top_maps,
    slot_nodes,
    slot_counts,
    top_loads,
    top_inverse,
):
    leaf_count = loads.shape[3]
    node_count = loads.shape[4]
    rhs_count = loads.shape[5]
    sep_width = chain_maps.shape[-1]
    slot_total = slot_nodes.shape[-1]
    largest_level = lax.Precision.HIGHEST
    local_loads = loads.reshape(leaf_count, node_count, rhs_count)
    flattened = loads.reshape(leaf_count * node_count, rhs_count)
    fluxes = jnp.dot(
        flux_maps.reshape(sep_width, leaf_count * node_count),
        flattened,
        preferred_element_type=jnp.float32,
    )
    combine_operator = chain_maps.reshape(sep_width, sep_width)
    chain_index = lax.axis_index("leaf")

    def advance(step_index, carried):
        earlier = passed_along(carried, "leaf", 1)
        advanced = (
            jnp.dot(
                combine_operator,
                earlier,
                precision=largest_level,
                preferred_element_type=jnp.float32,
            )
            + fluxes
        )
        return jnp.where(chain_index == step_index, advanced, carried)

    states = lax.fori_loop(1, lax.axis_size("leaf"), advance, fluxes)
    slot_ids = slot_nodes.reshape(slot_total)
    is_live = lax.iota(jnp.int32, slot_total) < slot_counts.reshape(())
    chosen_entries = jnp.where(is_live[:, None], states[:slot_total], jnp.float32(0.0))
    block_rows = top_loads.shape[0]
    row_ids = lax.iota(jnp.int32, block_rows * lax.axis_size("leaf"))
    match_table = (row_ids[:, None] == slot_ids[None, :]).astype(jnp.float32)
    top_block = lax.psum_scatter(
        jnp.dot(
            match_table, chosen_entries, precision=largest_level, preferred_element_type=jnp.float32
        ),
        "leaf",
        scatter_dimension=0,
        tiled=True,
    )
    top_block = lax.psum(top_block, ("row", "top"))
    rhs_block = top_loads - top_block
    column_rows = top_inverse.shape[1]
    rhs_piece = lax.dynamic_slice_in_dim(
        rhs_block, lax.axis_index("row") * column_rows, column_rows, 0
    )
    partial_value = jnp.dot(
        top_inverse, rhs_piece, precision=largest_level, preferred_element_type=jnp.float32
    )
    owned_rows = lax.psum(partial_value, ("leaf", "row"))
    shard_piece = lax.all_gather(owned_rows, "top", axis=0, tiled=True)
    row_ids = lax.iota(jnp.int32, shard_piece.shape[0])
    match_table = ((slot_ids[:, None] == row_ids[None, :]) & is_live[:, None]).astype(jnp.float32)
    boundary = jnp.dot(
        match_table, shard_piece, precision=largest_level, preferred_element_type=jnp.float32
    )
    states_low = states.astype(jnp.bfloat16)
    boundary_low = boundary.astype(jnp.bfloat16)
    summed = jnp.einsum(
        "lij,ljr->lir",
        leaf_maps.reshape(leaf_count, node_count, node_count),
        local_loads,
        preferred_element_type=jnp.float32,
    )
    summed = summed + jnp.einsum(
        "lik,kr->lir",
        edge_maps.reshape(leaf_count, node_count, sep_width),
        states_low,
        preferred_element_type=jnp.float32,
    )
    summed = summed + jnp.einsum(
        "lic,cr->lir",
        top_maps.reshape(leaf_count, node_count, slot_total),
        boundary_low,
        preferred_element_type=jnp.float32,
    )
    solution = summed.astype(jnp.bfloat16).reshape(1, 1, 1, leaf_count, node_count, rhs_count)
    return (solution, owned_rows)


def solution(mesh):
    in_specs = (
        P("leaf", "row", "top", None, None, None),
        P("leaf", "row", "top", None, None),
        P("leaf", "row", "top", None, None),
        P("leaf", "row", "top", None, None, None),
        P("leaf", "row", "top", None, None, None),
        P("leaf", "row", "top", None, None, None),
        P("leaf", "row", "top", None),
        P("leaf", "row", "top"),
        P("leaf", None),
        P("top", ("leaf", "row")),
    )
    out_specs = (P("leaf", "row", "top", None, None, None), P("top", None))
    return jax.shard_map(body, mesh=mesh, in_specs=in_specs, out_specs=out_specs, check_vma=False)
```

profile of v0, /device:TPU:0, one launch (start us, length us, event | category | flops | bytes accessed | tf_op | source)
XLA Modules:
  0.0 237.6 jit_solution(16142841711911786712)
XLA Ops:
  7.2 0.0 copy-start
  7.2 0.0 reduce-scatter.2.cloned.1.call-start
  7.9 0.2 copy-done
  8.2 0.9 fusion.15
  9.1 0.0 copy-start.7
  9.1 0.0 copy-start.4
  9.1 29.0 %while.13 = (s32[]{:T(128)}, f32[640,32]{0,1:T(8,128)S(1)}, s32[]{:T(128)}, f32[640,640]{1,0:T(8,128)}, f32[640,32]{0,1:T(8,128)S(1)}, /*index=5*/s32[]{:T(128)}) while((s32[]{:T(128)}, f32[640,32]{0,1:T(8,128)S(1)}, s32[]{:T(128)}, f32[640,640]{1,0:T(8,128)}, f32[640,32]{0,1:T(8,128)S(1)}, /*index=5*/s32[]{:T(128)}) %tuple.44), condition=%wide.region_1.2_spmd, body=%wide.region_0.1_spmd.sunk | while | flops 157327360 | bytes 2293879 | solution.py:54
  9.1 5.1 %collective-permute-start = (f32[640,32]{0,1:T(8,128)S(1)}, f32[640,32]{0,1:T(8,128)S(1)}, u32[]{:S(2)}, u32[]{:S(2)}) collective-permute-start(f32[640,32]{0,1:T(8,128)S(1)} %get-tuple-element.145), channel_id=1, source_target_pairs={{0,8},{8,16},{16,24},{1,9},{9,17},{17,25},{2,10},{10,18},{18,26},{... | collective-permute-start | bytes 245768 | tf_op jit(solution)/shard_map/while/body/eval_jaxpr/ppermute | solution.py:10
  14.2 2.0 collective-permute-done
  16.3 3.1 %fusion.39 = f32[640,32]{0,1:T(8,128)S(1)} fusion(f32[640,32]{0,1:T(8,128)S(1)} %get-tuple-element.145, f32[640,32]{0,1:T(8,128)S(1)} %get-tuple-element.154, f32[640,640]{1,0:T(8,128)} %get-tuple-element.153, f32[640,32]{0,1:T(8,128)S(1)} %collective-permute-done, pred[]{:T(512)S(6)} %eq.69), kind=kOutput, calls=%fused_computation.1.clone.1 | convolution fusion | flops 157327360 | bytes 1966081 | tf_op jit(solution)/shard_map/while/body/eval_jaxpr/dot_general | solution.py:44
  19.4 4.3 %collective-permute-start = (f32[640,32]{0,1:T(8,128)S(1)}, f32[640,32]{0,1:T(8,128)S(1)}, u32[]{:S(2)}, u32[]{:S(2)}) collective-permute-start(f32[640,32]{0,1:T(8,128)S(1)} %get-tuple-element.145), channel_id=1, source_target_pairs={{0,8},{8,16},{16,24},{1,9},{9,17},{17,25},{2,10},{10,18},{18,26},{... | collective-permute-start | bytes 245768 | tf_op jit(solution)/shard_map/while/body/eval_jaxpr/ppermute | solution.py:10
  23.7 2.0 collective-permute-done
  25.7 3.1 %fusion.39 = f32[640,32]{0,1:T(8,128)S(1)} fusion(f32[640,32]{0,1:T(8,128)S(1)} %get-tuple-element.145, f32[640,32]{0,1:T(8,128)S(1)} %get-tuple-element.154, f32[640,640]{1,0:T(8,128)} %get-tuple-element.153, f32[640,32]{0,1:T(8,128)S(1)} %collective-permute-done, pred[]{:T(512)S(6)} %eq.69), kind=kOutput, calls=%fused_computation.1.clone.1 | convolution fusion | flops 157327360 | bytes 1966081 | tf_op jit(solution)/shard_map/while/body/eval_jaxpr/dot_general | solution.py:44
  28.8 4.3 %collective-permute-start = (f32[640,32]{0,1:T(8,128)S(1)}, f32[640,32]{0,1:T(8,128)S(1)}, u32[]{:S(2)}, u32[]{:S(2)}) collective-permute-start(f32[640,32]{0,1:T(8,128)S(1)} %get-tuple-element.145), channel_id=1, source_target_pairs={{0,8},{8,16},{16,24},{1,9},{9,17},{17,25},{2,10},{10,18},{18,26},{... | collective-permute-start | bytes 245768 | tf_op jit(solution)/shard_map/while/body/eval_jaxpr/ppermute | solution.py:10
  33.1 2.0 collective-permute-done
  35.1 3.1 %fusion.39 = f32[640,32]{0,1:T(8,128)S(1)} fusion(f32[640,32]{0,1:T(8,128)S(1)} %get-tuple-element.145, f32[640,32]{0,1:T(8,128)S(1)} %get-tuple-element.154, f32[640,640]{1,0:T(8,128)} %get-tuple-element.153, f32[640,32]{0,1:T(8,128)S(1)} %collective-permute-done, pred[]{:T(512)S(6)} %eq.69), kind=kOutput, calls=%fused_computation.1.clone.1 | convolution fusion | flops 157327360 | bytes 1966081 | tf_op jit(solution)/shard_map/while/body/eval_jaxpr/dot_general | solution.py:44
  38.2 0.0 copy-done.7
  38.2 3.3 %fusion.2 = f32[8192,32]{0,1:T(8,128)} fusion(s32[128]{0:T(128)S(1)} %bitcast.45, f32[640,32]{0,1:T(8,128)S(1)} %get-tuple-element.96, pred[128]{0:T(512)(128)(4,1)S(1)} %iota_compare_fusion.3), kind=kOutput, calls=%fused_computation.5 | convolution fusion | flops 403705856 | bytes 1065984 | tf_op jit(solution)/shard_map/dot_general | solution.py:62
  41.5 0.0 reduce-scatter.2.cloned.1.call-update
  41.5 0.0 all-reduce.3.cloned.1.call-start
  41.6 29.4 %reduce-scatter.2.cloned.1.call-done = f32[2048,32]{0,1:T(8,128)} async-done(((f32[8192,32]{0,1:T(8,128)}), f32[2048,32]{0,1:T(8,128)}) %reduce-scatter.2.cloned.1.call-update) | async-done | bytes 262160 | tf_op jit(solution)/shard_map/reduce_scatter | solution.py:61
  71.0 0.0 all-reduce.3.cloned.1.call-update
  71.0 0.0 all-reduce.5.cloned.1.call-start
  71.1 0.0 copy-start.2
  71.1 0.0 copy-start.3
  71.1 0.0 copy-start.6
  71.1 55.4 %all-reduce.3.cloned.1.call-done = f32[2048,32]{0,1:T(8,128)} async-done(((f32[2048,32]{0,1:T(8,128)}), f32[2048,32]{0,1:T(8,128)}) %all-reduce.3.cloned.1.call-update) | async-done | bytes 262160 | tf_op jit(solution)/shard_map/psum | solution.py:69
  126.5 0.0 copy-done.4
  126.5 11.7 %convolution_bitcast_fusion = f32[2048,32]{0,1:T(8,128)} fusion(f32[2048,1024]{1,0:T(8,128)} %param.21, f32[2048,32]{0,1:T(8,128)} %all-reduce.3.cloned.1.call-done, s32[]{:T(128)S(6)} %select_n.24, f32[2048,32]{0,1:T(8,128)S(1)} %copy-done.4), kind=kOutput, calls=%fused_computation.7 | convolution fusion | flops 805339136 | bytes 8912900 | tf_op jit(solution)/shard_map/dot_general | solution.py:75
  138.2 0.0 copy-start.5
  138.2 0.0 all-reduce.5.cloned.1.call-update
  138.2 0.0 all-gather.2.cloned.1.call-start
  138.2 70.5 %all-reduce.5.cloned.1.call-done = f32[2048,32]{0,1:T(8,128)} async-done(((f32[2048,32]{0,1:T(8,128)}), f32[2048,32]{0,1:T(8,128)}) %all-reduce.5.cloned.1.call-update) | async-done | bytes 262160 | tf_op jit(solution)/shard_map/psum | solution.py:78
  208.7 0.0 copy-start.1
  208.7 0.0 all-gather.2.cloned.1.call-update
  208.8 0.0 copy-done.2
  208.8 0.2 convolution_bitcast_fusion.2
  208.9 0.0 copy-done.3
  209.0 0.0 copy-done.6
  209.0 0.2 convolution_add_fusion.1
  209.2 16.9 %all-gather.2.cloned.1.call-done = f32[8192,32]{0,1:T(8,128)} async-done(((f32[2048,32]{0,1:T(8,128)}), f32[8192,32]{0,1:T(8,128)}) %all-gather.2.cloned.1.call-update) | async-done | bytes 1048592 | tf_op jit(solution)/shard_map/all_gather | solution.py:79
  226.1 3.5 %fusion.8 = bf16[128,32]{1,0:T(8,128)(2,1)S(1)} fusion(f32[8192,32]{0,1:T(8,128)} %all-gather.2.cloned.1.call-done, s32[128]{0:T(128)S(1)} %bitcast.46, pred[128]{0:T(512)(128)(4,1)S(1)} %iota_compare_fusion.3), kind=kOutput, calls=%fused_computation.11 | convolution fusion | flops 404754432 | bytes 1057408 | tf_op jit(solution)/shard_map/dot_general | solution.py:82
  229.6 0.0 copy-done.5
  229.6 0.8 fusion.13
  230.4 0.0 copy-done.1
  230.4 0.7 copy.21
  (2 shorter events, 0.0 us)
Async XLA Ops:
  7.2 1.0 copy-start
  7.2 63.8 %reduce-scatter.2.cloned.1.call-start = ((), (), s32[]{:S(2)}) async-start(), calls=%async_computation.1 | async-start | bytes 1310720 | tf_op jit(solution)/shard_map/reduce_scatter | solution.py:61
  9.1 29.1 %copy-start.7 = (s32[1,1,1,128]{3,2,1,0:T(1,128)S(1)}, s32[1,1,1,128]{3,2,1,0:T(1,128)}, u32[]{:S(2)}) copy-start(s32[1,1,1,128]{3,2,1,0:T(1,128)} %param.18) | copy-start | bytes 1540
  9.1 117.4 %copy-start.4 = (f32[2048,32]{0,1:T(8,128)S(1)}, f32[2048,32]{0,1:T(8,128)}, u32[]{:S(2)}) copy-start(f32[2048,32]{0,1:T(8,128)} %param.20) | copy-start | bytes 786436
  9.1 7.1 %collective-permute-start = (f32[640,32]{0,1:T(8,128)S(1)}, f32[640,32]{0,1:T(8,128)S(1)}, u32[]{:S(2)}, u32[]{:S(2)}) collective-permute-start(f32[640,32]{0,1:T(8,128)S(1)} %get-tuple-element.145), channel_id=1, source_target_pairs={{0,8},{8,16},{16,24},{1,9},{9,17},{17,25},{2,10},{10,18},{18,26},{... | collective-permute-start | bytes 245768 | tf_op jit(solution)/shard_map/while/body/eval_jaxpr/ppermute | solution.py:10
  19.4 6.3 %collective-permute-start = (f32[640,32]{0,1:T(8,128)S(1)}, f32[640,32]{0,1:T(8,128)S(1)}, u32[]{:S(2)}, u32[]{:S(2)}) collective-permute-start(f32[640,32]{0,1:T(8,128)S(1)} %get-tuple-element.145), channel_id=1, source_target_pairs={{0,8},{8,16},{16,24},{1,9},{9,17},{17,25},{2,10},{10,18},{18,26},{... | collective-permute-start | bytes 245768 | tf_op jit(solution)/shard_map/while/body/eval_jaxpr/ppermute | solution.py:10
  28.8 6.3 %collective-permute-start = (f32[640,32]{0,1:T(8,128)S(1)}, f32[640,32]{0,1:T(8,128)S(1)}, u32[]{:S(2)}, u32[]{:S(2)}) collective-permute-start(f32[640,32]{0,1:T(8,128)S(1)} %get-tuple-element.145), channel_id=1, source_target_pairs={{0,8},{8,16},{16,24},{1,9},{9,17},{17,25},{2,10},{10,18},{18,26},{... | collective-permute-start | bytes 245768 | tf_op jit(solution)/shard_map/while/body/eval_jaxpr/ppermute | solution.py:10
  41.5 84.9 %all-reduce.3.cloned.1.call-start = ((), (), s32[]{:S(2)}) async-start(), calls=%async_computation.2 | async-start | bytes 524288 | tf_op jit(solution)/shard_map/psum | solution.py:69
  71.0 137.7 %all-reduce.5.cloned.1.call-start = ((), (), s32[]{:S(2)}) async-start(), calls=%async_computation.3 | async-start | bytes 524288 | tf_op jit(solution)/shard_map/psum | solution.py:78
  71.1 137.7 %copy-start.2 = (bf16[1,1,1,1,256,640]{5,4,3,2,1,0:T(8,128)(2,1)S(1)}, bf16[1,1,1,1,256,640]{5,4,3,2,1,0:T(8,128)(2,1)}, u32[]{:S(2)}) copy-start(bf16[1,1,1,1,256,640]{5,4,3,2,1,0:T(8,128)(2,1)} %param.16) | copy-start | bytes 983044
  71.1 137.9 %copy-start.3 = (bf16[1,1,1,1,256,256]{5,4,3,2,1,0:T(8,128)(2,1)S(1)}, bf16[1,1,1,1,256,256]{5,4,3,2,1,0:T(8,128)(2,1)}, u32[]{:S(2)}) copy-start(bf16[1,1,1,1,256,256]{5,4,3,2,1,0:T(8,128)(2,1)} %param.15) | copy-start | bytes 393220
  71.1 137.9 %copy-start.6 = (bf16[1,1,1,1,256,32]{4,5,3,2,1,0:T(8,128)(2,1)S(1)}, bf16[1,1,1,1,256,32]{4,5,3,2,1,0:T(8,128)(2,1)}, u32[]{:S(2)}) copy-start(bf16[1,1,1,1,256,32]{4,5,3,2,1,0:T(8,128)(2,1)} %param.12) | copy-start | bytes 49156
  138.2 91.4 %copy-start.5 = (bf16[1,1,1,1,256,128]{5,4,3,2,1,0:T(8,128)(2,1)S(1)}, bf16[1,1,1,1,256,128]{5,4,3,2,1,0:T(8,128)(2,1)}, u32[]{:S(2)}) copy-start(bf16[1,1,1,1,256,128]{5,4,3,2,1,0:T(8,128)(2,1)} %param.17) | copy-start | bytes 196612
  138.2 87.9 %all-gather.2.cloned.1.call-start = ((), (), s32[]{:S(2)}) async-start(), calls=%async_computation.4 | async-start | bytes 1310720 | tf_op jit(solution)/shard_map/all_gather | solution.py:79
  208.7 21.6 %copy-start.1 = (f32[2048,32]{0,1:T(8,128)S(1)}, f32[2048,32]{0,1:T(8,128)}, u32[]{:S(2)}) copy-start(f32[2048,32]{0,1:T(8,128)} %all-reduce.5.cloned.1.call-done) | copy-start | bytes 786436
Sparse Core Ops, SparseCore 0:
  41.6 29.3 reduce-scatter.1
  74.1 52.3 all-reduce.2
  138.3 70.3 all-reduce.4
  210.2 15.8 all-gather.1
where the time goes:
time: 238 us
  waiting for transfers between devices  178 us (75%)
  matrix products  29.7 us (12%)
  between operations  14.6 us (6%)
  starting transfers between devices  13.8 us (6%)
    psum x1, waiting for transfers between devices, body(): owned_rows = lax.psum(partial_value, ('leaf', 'row'))  70.5 us
    psum x1, waiting for transfers between devices, body(): top_block = lax.psum(top_block, ('row', 'top'))  55.4 us
    reduce_scatter x1, waiting for transfers between devices, body(): lax.psum_scatter(jnp.dot(match_table, chosen_entries, precision=largest_l...  29.4 us
    all_gather x1, waiting for transfers between devices, body(): shard_piece = lax.all_gather(owned_rows, 'top', axis=0, tiled=True)  16.9 us
    ppermute x3, starting transfers between devices, passed_along(): lax.ppermute(value, axis, [(source, source + steps) for source in range(f...  13.7 us
    dot_general x1, matrix products, body(): jnp.dot(top_inverse, rhs_piece, precision=largest_level, preferred_elemen...  11.7 us
    dot_general x3, matrix products, advance(): jnp.dot(combine_operator, earlier, precision=largest_level, preferred_ele...  9.17 us
    ppermute x3, waiting for transfers between devices, passed_along(): lax.ppermute(value, axis, [(source, source + steps) for source in range(f...  6.09 us
  transfers between devices with their start and end apart: 7, of which 7 were waited for; matrix products, arithmetic and copies ran while one was open for 0% of the time, Pallas kernels for 0%

commit v1 on v0

--- a/solution.py
+++ b/solution.py
@@ -2,6 +2,23 @@
 import jax.numpy as jnp
 from jax import lax
 from jax.sharding import PartitionSpec as P
+
+
+def in_order(tiles, dim):
+    tiles = jnp.moveaxis(tiles, 0, dim)
+    shape = tiles.shape
+    return tiles.reshape(*shape[:dim], shape[dim] * shape[dim + 1], *shape[dim + 2 :])
+
+
+def ring_gather(x, axis, dim):
+    peers = lax.axis_size(axis)
+    ahead = [(i, (i + 1) % peers) for i in range(peers)]
+    tiles = [x]
+    while len(tiles) < peers:
+        tiles.append(lax.ppermute(tiles[-1], axis, ahead))
+    mine = lax.axis_index(axis)
+    tiles = jnp.stack(tiles)[(mine - jnp.arange(peers)) % peers]
+    return in_order(tiles, dim)
 
 
 def passed_along(value, axis, steps):
@@ -76,7 +93,7 @@
         top_inverse, rhs_piece, precision=largest_level, preferred_element_type=jnp.float32
     )
     owned_rows = lax.psum(partial_value, ("leaf", "row"))
-    shard_piece = lax.all_gather(owned_rows, "top", axis=0, tiled=True)
+    shard_piece = ring_gather(owned_rows, "top", 0)
     row_ids = lax.iota(jnp.int32, shard_piece.shape[0])
     match_table = ((slot_ids[:, None] == row_ids[None, :]) & is_live[:, None]).astype(jnp.float32)
     boundary = jnp.dot(

time: 238 us -> 239 us (level)
    ppermute x0 -> x3, waiting for transfers between devices: none -> 17.2 us  [ring_gather(): tiles.append(lax.ppermute(tiles[-1], axis, ahead))]
    all_gather x1 -> x0, waiting for transfers between devices: 16.9 us -> none  [body(): shard_piece = lax.all_gather(owned_rows, 'top', axis=0, tiled=True)]
  transfers between devices with their start and end apart: 7 -> 9, of which waited for: 7 -> 9; matrix products, arithmetic and copies ran while one was open for 0% -> 0% of each run, Pallas kernels for 0% -> 0%
where the time goes in v1:
time: 239 us; the launch traced here: 238 us
  waiting for transfers between devices  179 us (75%)
  matrix products  28.4 us (12%)
  between operations  14.6 us (6%)
  starting transfers between devices  13.8 us (6%)
    psum x1, waiting for transfers between devices, body(): owned_rows = lax.psum(partial_value, ('leaf', 'row'))  70.6 us
    psum x1, waiting for transfers between devices, body(): top_block = lax.psum(top_block, ('row', 'top'))  55.4 us
    reduce_scatter x1, waiting for transfers between devices, body(): lax.psum_scatter(jnp.dot(match_table, chosen_entries, precision=largest_l...  29.4 us
    ppermute x3, waiting for transfers between devices, ring_gather(): tiles.append(lax.ppermute(tiles[-1], axis, ahead))  17.2 us
    ppermute x3, starting transfers between devices, passed_along(): lax.ppermute(value, axis, [(source, source + steps) for source in range(f...  13.7 us
    dot_general x1, matrix products, body(): jnp.dot(top_inverse, rhs_piece, precision=largest_level, preferred_elemen...  11.7 us
    dot_general x3, matrix products, advance(): jnp.dot(combine_operator, earlier, precision=largest_level, preferred_ele...  9.16 us
    ppermute x3, waiting for transfers between devices, passed_along(): lax.ppermute(value, axis, [(source, source + steps) for source in range(f...  6.09 us
  transfers between devices with their start and end apart: 9, of which 9 were waited for; matrix products, arithmetic and copies ran while one was open for 0% of the time, Pallas kernels for 0%

profile of v1, /device:TPU:0, one launch (start us, length us, event | category | flops | bytes accessed | tf_op | source)
XLA Modules:
  0.0 238.4 jit_solution(14037981721983109082)
XLA Ops:
  7.2 0.0 copy-start
  7.2 0.0 reduce-scatter.2.cloned.1.call-start
  7.9 0.2 copy-done
  8.2 0.9 fusion.15
  9.1 0.0 copy-start.7
  9.1 0.0 copy-start.4
  9.1 29.0 %while.13 = (s32[]{:T(128)}, f32[640,32]{0,1:T(8,128)S(1)}, s32[]{:T(128)}, f32[640,640]{1,0:T(8,128)}, f32[640,32]{0,1:T(8,128)S(1)}, /*index=5*/s32[]{:T(128)}) while((s32[]{:T(128)}, f32[640,32]{0,1:T(8,128)S(1)}, s32[]{:T(128)}, f32[640,640]{1,0:T(8,128)}, f32[640,32]{0,1:T(8,128)S(1)}, /*index=5*/s32[]{:T(128)}) %tuple.42), condition=%wide.region_1.2_spmd, body=%wide.region_0.1_spmd.sunk | while | flops 157327360 | bytes 2293879 | solution.py:71
  9.1 5.1 %collective-permute-start = (f32[640,32]{0,1:T(8,128)S(1)}, f32[640,32]{0,1:T(8,128)S(1)}, u32[]{:S(2)}, u32[]{:S(2)}) collective-permute-start(f32[640,32]{0,1:T(8,128)S(1)} %get-tuple-element.145), channel_id=1, source_target_pairs={{0,8},{8,16},{16,24},{1,9},{9,17},{17,25},{2,10},{10,18},{18,26},{... | collective-permute-start | bytes 245768 | tf_op jit(solution)/shard_map/while/body/eval_jaxpr/ppermute | solution.py:27
  14.2 2.0 collective-permute-done
  16.3 3.1 %fusion.41 = f32[640,32]{0,1:T(8,128)S(1)} fusion(f32[640,32]{0,1:T(8,128)S(1)} %get-tuple-element.145, f32[640,32]{0,1:T(8,128)S(1)} %get-tuple-element.154, f32[640,640]{1,0:T(8,128)} %get-tuple-element.153, f32[640,32]{0,1:T(8,128)S(1)} %collective-permute-done, pred[]{:T(512)S(6)} %eq.71), kind=kOutput, calls=%fused_computation.2.clone.1 | convolution fusion | flops 157327360 | bytes 1966081 | tf_op jit(solution)/shard_map/while/body/eval_jaxpr/dot_general | solution.py:61
  19.4 4.3 %collective-permute-start = (f32[640,32]{0,1:T(8,128)S(1)}, f32[640,32]{0,1:T(8,128)S(1)}, u32[]{:S(2)}, u32[]{:S(2)}) collective-permute-start(f32[640,32]{0,1:T(8,128)S(1)} %get-tuple-element.145), channel_id=1, source_target_pairs={{0,8},{8,16},{16,24},{1,9},{9,17},{17,25},{2,10},{10,18},{18,26},{... | collective-permute-start | bytes 245768 | tf_op jit(solution)/shard_map/while/body/eval_jaxpr/ppermute | solution.py:27
  23.7 2.0 collective-permute-done
  25.7 3.1 %fusion.41 = f32[640,32]{0,1:T(8,128)S(1)} fusion(f32[640,32]{0,1:T(8,128)S(1)} %get-tuple-element.145, f32[640,32]{0,1:T(8,128)S(1)} %get-tuple-element.154, f32[640,640]{1,0:T(8,128)} %get-tuple-element.153, f32[640,32]{0,1:T(8,128)S(1)} %collective-permute-done, pred[]{:T(512)S(6)} %eq.71), kind=kOutput, calls=%fused_computation.2.clone.1 | convolution fusion | flops 157327360 | bytes 1966081 | tf_op jit(solution)/shard_map/while/body/eval_jaxpr/dot_general | solution.py:61
  28.8 4.3 %collective-permute-start = (f32[640,32]{0,1:T(8,128)S(1)}, f32[640,32]{0,1:T(8,128)S(1)}, u32[]{:S(2)}, u32[]{:S(2)}) collective-permute-start(f32[640,32]{0,1:T(8,128)S(1)} %get-tuple-element.145), channel_id=1, source_target_pairs={{0,8},{8,16},{16,24},{1,9},{9,17},{17,25},{2,10},{10,18},{18,26},{... | collective-permute-start | bytes 245768 | tf_op jit(solution)/shard_map/while/body/eval_jaxpr/ppermute | solution.py:27
  33.1 2.0 collective-permute-done
  35.1 3.1 %fusion.41 = f32[640,32]{0,1:T(8,128)S(1)} fusion(f32[640,32]{0,1:T(8,128)S(1)} %get-tuple-element.145, f32[640,32]{0,1:T(8,128)S(1)} %get-tuple-element.154, f32[640,640]{1,0:T(8,128)} %get-tuple-element.153, f32[640,32]{0,1:T(8,128)S(1)} %collective-permute-done, pred[]{:T(512)S(6)} %eq.71), kind=kOutput, calls=%fused_computation.2.clone.1 | convolution fusion | flops 157327360 | bytes 1966081 | tf_op jit(solution)/shard_map/while/body/eval_jaxpr/dot_general | solution.py:61
  38.2 0.0 copy-done.7
  38.2 3.3 %fusion.2 = f32[8192,32]{0,1:T(8,128)} fusion(s32[128]{0:T(128)S(1)} %bitcast.59, f32[640,32]{0,1:T(8,128)S(1)} %get-tuple-element.96, pred[128]{0:T(512)(128)(4,1)S(1)} %iota_compare_fusion.3), kind=kOutput, calls=%fused_computation.6 | convolution fusion | flops 403705856 | bytes 1065984 | tf_op jit(solution)/shard_map/dot_general | solution.py:79
  41.5 0.0 reduce-scatter.2.cloned.1.call-update
  41.5 0.0 all-reduce.3.cloned.1.call-start
  41.6 29.4 %reduce-scatter.2.cloned.1.call-done = f32[2048,32]{0,1:T(8,128)} async-done(((f32[8192,32]{0,1:T(8,128)}), f32[2048,32]{0,1:T(8,128)}) %reduce-scatter.2.cloned.1.call-update) | async-done | bytes 262160 | tf_op jit(solution)/shard_map/reduce_scatter | solution.py:78
  71.0 0.0 all-reduce.3.cloned.1.call-update
  71.0 0.0 all-reduce.5.cloned.1.call-start
  71.1 0.0 copy-start.2
  71.1 0.0 copy-start.3
  71.1 0.0 copy-start.6
  71.1 55.4 %all-reduce.3.cloned.1.call-done = f32[2048,32]{0,1:T(8,128)} async-done(((f32[2048,32]{0,1:T(8,128)}), f32[2048,32]{0,1:T(8,128)}) %all-reduce.3.cloned.1.call-update) | async-done | bytes 262160 | tf_op jit(solution)/shard_map/psum | solution.py:86
  126.5 0.0 copy-done.4
  126.5 11.7 %convolution_bitcast_fusion = f32[2048,32]{0,1:T(8,128)} fusion(f32[2048,1024]{1,0:T(8,128)} %param.21, f32[2048,32]{0,1:T(8,128)} %all-reduce.3.cloned.1.call-done, s32[]{:T(128)S(6)} %select_n.48, f32[2048,32]{0,1:T(8,128)S(1)} %copy-done.4), kind=kOutput, calls=%fused_computation.8 | convolution fusion | flops 805339136 | bytes 8912900 | tf_op jit(solution)/shard_map/dot_general | solution.py:92
  138.1 0.0 all-reduce.5.cloned.1.call-update
  138.2 70.6 %all-reduce.5.cloned.1.call-done = f32[2048,32]{0,1:T(8,128)} async-done(((f32[2048,32]{0,1:T(8,128)}), f32[2048,32]{0,1:T(8,128)}) %all-reduce.5.cloned.1.call-update) | async-done | bytes 262160 | tf_op jit(solution)/shard_map/psum | solution.py:95
  208.7 0.0 collective-permute-start.1
  208.7 6.0 %collective-permute-done.1 = f32[2048,32]{0,1:T(8,128)S(1)} collective-permute-done((f32[2048,32]{0,1:T(8,128)}, f32[2048,32]{0,1:T(8,128)S(1)}, u32[]{:S(2)}, u32[]{:S(2)}) %collective-permute-start.1) | collective-permute-done | bytes 262176 | tf_op jit(solution)/shard_map/ppermute | solution.py:18
  214.7 0.0 collective-permute-start.2
  214.7 0.0 copy-done.2
  214.8 0.2 convolution_bitcast_fusion.2
  214.9 5.6 %collective-permute-done.2 = f32[2048,32]{0,1:T(8,128)S(1)} collective-permute-done((f32[2048,32]{0,1:T(8,128)S(1)}, f32[2048,32]{0,1:T(8,128)S(1)}, u32[]{:S(2)}, u32[]{:S(2)}) %collective-permute-start.2) | collective-permute-done | bytes 262176 | tf_op jit(solution)/shard_map/ppermute | solution.py:18
  220.5 0.0 collective-permute-start.3
  220.5 0.0 copy-done.3
  220.5 0.0 copy-done.6
  220.6 0.2 convolution_add_fusion.1
  220.7 5.6 %collective-permute-done.3 = f32[2048,32]{0,1:T(8,128)S(1)} collective-permute-done((f32[2048,32]{0,1:T(8,128)S(1)}, f32[2048,32]{0,1:T(8,128)S(1)}, u32[]{:S(2)}, u32[]{:S(2)}) %collective-permute-start.3) | collective-permute-done | bytes 262176 | tf_op jit(solution)/shard_map/ppermute | solution.py:18
  226.3 1.0 pad_maximum_fusion
  227.3 0.6 gather_fusion
  228.0 0.0 copy-start.5
  228.0 0.0 copy-start.1
  228.0 0.1 copy.13
  228.1 2.3 fusion.8
  230.3 0.0 copy-done.5
  230.3 0.8 fusion.13
  231.1 0.0 copy-done.1
  231.1 0.7 copy.23
  (4 shorter events, 0.1 us)
Async XLA Ops:
  7.2 1.0 copy-start
  7.2 63.8 %reduce-scatter.2.cloned.1.call-start = ((), (), s32[]{:S(2)}) async-start(), calls=%async_computation.1 | async-start | bytes 1310720 | tf_op jit(solution)/shard_map/reduce_scatter | solution.py:78
  9.1 29.1 %copy-start.7 = (s32[1,1,1,128]{3,2,1,0:T(1,128)S(1)}, s32[1,1,1,128]{3,2,1,0:T(1,128)}, u32[]{:S(2)}) copy-start(s32[1,1,1,128]{3,2,1,0:T(1,128)} %param.18) | copy-start | bytes 1540
  9.1 117.3 %copy-start.4 = (f32[2048,32]{0,1:T(8,128)S(1)}, f32[2048,32]{0,1:T(8,128)}, u32[]{:S(2)}) copy-start(f32[2048,32]{0,1:T(8,128)} %param.20) | copy-start | bytes 786436
  9.1 7.1 %collective-permute-start = (f32[640,32]{0,1:T(8,128)S(1)}, f32[640,32]{0,1:T(8,128)S(1)}, u32[]{:S(2)}, u32[]{:S(2)}) collective-permute-start(f32[640,32]{0,1:T(8,128)S(1)} %get-tuple-element.145), channel_id=1, source_target_pairs={{0,8},{8,16},{16,24},{1,9},{9,17},{17,25},{2,10},{10,18},{18,26},{... | collective-permute-start | bytes 245768 | tf_op jit(solution)/shard_map/while/body/eval_jaxpr/ppermute | solution.py:27
  19.4 6.3 %collective-permute-start = (f32[640,32]{0,1:T(8,128)S(1)}, f32[640,32]{0,1:T(8,128)S(1)}, u32[]{:S(2)}, u32[]{:S(2)}) collective-permute-start(f32[640,32]{0,1:T(8,128)S(1)} %get-tuple-element.145), channel_id=1, source_target_pairs={{0,8},{8,16},{16,24},{1,9},{9,17},{17,25},{2,10},{10,18},{18,26},{... | collective-permute-start | bytes 245768 | tf_op jit(solution)/shard_map/while/body/eval_jaxpr/ppermute | solution.py:27
  28.8 6.3 %collective-permute-start = (f32[640,32]{0,1:T(8,128)S(1)}, f32[640,32]{0,1:T(8,128)S(1)}, u32[]{:S(2)}, u32[]{:S(2)}) collective-permute-start(f32[640,32]{0,1:T(8,128)S(1)} %get-tuple-element.145), channel_id=1, source_target_pairs={{0,8},{8,16},{16,24},{1,9},{9,17},{17,25},{2,10},{10,18},{18,26},{... | collective-permute-start | bytes 245768 | tf_op jit(solution)/shard_map/while/body/eval_jaxpr/ppermute | solution.py:27
  41.5 84.9 %all-reduce.3.cloned.1.call-start = ((), (), s32[]{:S(2)}) async-start(), calls=%async_computation.2 | async-start | bytes 524288 | tf_op jit(solution)/shard_map/psum | solution.py:86
  71.0 137.7 %all-reduce.5.cloned.1.call-start = ((), (), s32[]{:S(2)}) async-start(), calls=%async_computation.3 | async-start | bytes 524288 | tf_op jit(solution)/shard_map/psum | solution.py:95
  71.1 143.7 %copy-start.2 = (bf16[1,1,1,1,256,640]{5,4,3,2,1,0:T(8,128)(2,1)S(1)}, bf16[1,1,1,1,256,640]{5,4,3,2,1,0:T(8,128)(2,1)}, u32[]{:S(2)}) copy-start(bf16[1,1,1,1,256,640]{5,4,3,2,1,0:T(8,128)(2,1)} %param.16) | copy-start | bytes 983044
  71.1 149.5 %copy-start.3 = (bf16[1,1,1,1,256,256]{5,4,3,2,1,0:T(8,128)(2,1)S(1)}, bf16[1,1,1,1,256,256]{5,4,3,2,1,0:T(8,128)(2,1)}, u32[]{:S(2)}) copy-start(bf16[1,1,1,1,256,256]{5,4,3,2,1,0:T(8,128)(2,1)} %param.15) | copy-start | bytes 393220
  71.1 149.5 %copy-start.6 = (bf16[1,1,1,1,256,32]{4,5,3,2,1,0:T(8,128)(2,1)S(1)}, bf16[1,1,1,1,256,32]{4,5,3,2,1,0:T(8,128)(2,1)}, u32[]{:S(2)}) copy-start(bf16[1,1,1,1,256,32]{4,5,3,2,1,0:T(8,128)(2,1)} %param.12) | copy-start | bytes 49156
  208.7 6.0 %collective-permute-start.1 = (f32[2048,32]{0,1:T(8,128)}, f32[2048,32]{0,1:T(8,128)S(1)}, u32[]{:S(2)}, u32[]{:S(2)}) collective-permute-start(f32[2048,32]{0,1:T(8,128)} %all-reduce.5.cloned.1.call-done), channel_id=1, source_target_pairs={{0,1},{1,2},{2,3},{3,0},{4,5},{5,6},{6,7},{7,4},{8,9},{9,10},{10,1... | collective-permute-start | bytes 786440 | tf_op jit(solution)/shard_map/ppermute | solution.py:18
  214.7 5.8 %collective-permute-start.2 = (f32[2048,32]{0,1:T(8,128)S(1)}, f32[2048,32]{0,1:T(8,128)S(1)}, u32[]{:S(2)}, u32[]{:S(2)}) collective-permute-start(f32[2048,32]{0,1:T(8,128)S(1)} %collective-permute-done.1), channel_id=1, source_target_pairs={{0,1},{1,2},{2,3},{3,0},{4,5},{5,6},{6,7},{7,4},{8,9},{9,10},{10,1... | collective-permute-start | bytes 786440 | tf_op jit(solution)/shard_map/ppermute | solution.py:18
  220.5 5.8 %collective-permute-start.3 = (f32[2048,32]{0,1:T(8,128)S(1)}, f32[2048,32]{0,1:T(8,128)S(1)}, u32[]{:S(2)}, u32[]{:S(2)}) collective-permute-start(f32[2048,32]{0,1:T(8,128)S(1)} %collective-permute-done.2), channel_id=1, source_target_pairs={{0,1},{1,2},{2,3},{3,0},{4,5},{5,6},{6,7},{7,4},{8,9},{9,10},{10,1... | collective-permute-start | bytes 786440 | tf_op jit(solution)/shard_map/ppermute | solution.py:18
  228.0 2.4 copy-start.5
  228.0 3.1 %copy-start.1 = (f32[2048,32]{0,1:T(8,128)S(1)}, f32[2048,32]{0,1:T(8,128)}, u32[]{:S(2)}) copy-start(f32[2048,32]{0,1:T(8,128)} %all-reduce.5.cloned.1.call-done) | copy-start | bytes 786436
Sparse Core Ops, SparseCore 0:
  41.6 29.3 reduce-scatter.1
  74.0 52.3 all-reduce.2
  138.3 70.3 all-reduce.4
